TPU v7x, 512 devices: a whole 4x4x16 slice. The times are simulated.
512 devices in a mesh: ad: 64 (over z, x), tp: 8 (over y, core).
Axes of the slice: x: 4, y: 4, z: 16, core: 2. Of those that a mesh axis runs over, the one named last changes fastest.
Arguments:
- tokens: bfloat16 [4, 3072, 8192], P(None, 'ad', 'tp'), may hold values from -6 to 6
- row_adapter_index: int32 [4, 3072], P(None, 'ad'), may hold values from 0 to 255, as said below
- key_base_weight: bfloat16 [8192, 1024], P('tp'), may hold values from -0.0625 to 0.0625
- adapter_down_weight: bfloat16 [256, 8192, 64], P('ad', 'tp'), may hold values from -0.0625 to 0.0625
- adapter_up_weight: bfloat16 [256, 64, 1024], P('ad', None, 'tp'), may hold values from -0.75 to 0.75
Outputs:
- token_keys_output: bfloat16 [4, 3072, 1024], P(None, 'ad', 'tp')
Inputs may be any that keep to these rules, and one draw needn't show every extreme that they name: `row_adapter_index`: group g holds adapters g * 4 to (g + 1) * 4 - 1. In each step the 48 rows of one index of ad name one group in exactly 2 rows and every other group in at most 1 row; that busiest group is the same for every index of ad in a step, so it receives 2 rows from each.
All inputs are finite; a program needn't handle non-finite values.
Results may differ from a plain program's by a relative error of at most 0.005.
Values may be sent and summed in bfloat16 or wider, within the bound.
A program may use at most 64 MiB of HBM per device.

v0:
```python
import jax
import jax.numpy as jnp
from jax import lax
from jax.sharding import PartitionSpec as P

TAG_WIDTH = 128


def body(tokens, row_adapter_index, key_base_weight, adapter_down_weight, adapter_up_weight):
    step_count, row_dev, width_per_shard = tokens.shape
    groups = lax.axis_size("ad")
    me = lax.axis_index("ad")
    adapter_number = adapter_down_weight.shape[0]
    rank = adapter_down_weight.shape[2]
    row_total = step_count * row_dev
    regular_total = groups * step_count
    wide = width_per_shard + TAG_WIDTH
    gathered_rows = tokens.reshape(row_total, width_per_shard)
    index_list = row_adapter_index.reshape(step_count, row_dev)
    owner_group = index_list // adapter_number
    local_index = index_list % adapter_number
    group_hits = (
        owner_group[:, :, None] == jnp.arange(groups, dtype=jnp.int32)[None, None, :]
    ).astype(jnp.int32)
    slot_rank = jnp.sum((jnp.cumsum(group_hits, axis=1) - group_hits) * group_hits, axis=2)
    step_ids = jnp.arange(step_count, dtype=jnp.int32)[:, None]
    first = slot_rank == 0
    regular_slot = jnp.where(first, owner_group * step_count + step_ids, -1).reshape(row_total)
    overflow_slot = jnp.where(slot_rank == 1, step_ids, -1).reshape(row_total)
    dispatch = (
        regular_slot[None, :] == jnp.arange(regular_total, dtype=jnp.int32)[:, None]
    ).astype(jnp.bfloat16)
    dispatch_over = (
        overflow_slot[None, :] == jnp.arange(step_count, dtype=jnp.int32)[:, None]
    ).astype(jnp.bfloat16)
    tag_values = jnp.where(first, local_index + 1, index_list + 1).astype(jnp.bfloat16)
    tag_block = jnp.broadcast_to(tag_values.reshape(row_total, 1), (row_total, TAG_WIDTH))
    rows_tagged = jnp.concatenate([gathered_rows, tag_block], axis=1)
    send_rows = jnp.dot(dispatch, rows_tagged, preferred_element_type=jnp.float32).astype(
        jnp.bfloat16
    )
    send_rows = send_rows.reshape(groups, step_count, wide)
    send_over = jnp.dot(dispatch_over, rows_tagged, preferred_element_type=jnp.float32).astype(
        jnp.bfloat16
    )
    incoming_over = lax.all_gather(send_over, "ad", tiled=True)
    incoming = lax.all_to_all(send_rows, "ad", split_axis=0, concat_axis=0, tiled=True)
    partial_base = jnp.dot(gathered_rows, key_base_weight, preferred_element_type=jnp.float32)
    partial_base, incoming_over = lax.optimization_barrier((partial_base, incoming_over))
    base_keys_output = lax.psum_scatter(partial_base, "tp", scatter_dimension=1, tiled=True)
    key_feature_width = base_keys_output.shape[1]
    incoming = jnp.concatenate([incoming.reshape(regular_total, wide), incoming_over], axis=0)
    slot_total = incoming.shape[0]
    incoming_rows = incoming[:, :width_per_shard]
    regular_labels = incoming[:regular_total, width_per_shard].astype(jnp.float32)
    over_labels = incoming[regular_total:, width_per_shard].astype(jnp.float32) - (
        me * adapter_number
    ).astype(jnp.float32)
    incoming_labels = jnp.concatenate([regular_labels, over_labels])
    down_all = jnp.einsum(
        "nd,adr->nar", incoming_rows, adapter_down_weight, preferred_element_type=jnp.float32
    )
    labels = (jnp.arange(adapter_number, dtype=jnp.int32) + 1).astype(jnp.float32)
    selector = (incoming_labels[:, None] == labels[None, :]).astype(jnp.float32)
    down_part = jnp.sum(down_all * selector[:, :, None], axis=1)
    down_sum = lax.psum(down_part, "tp")
    down_low = down_sum.astype(jnp.bfloat16)
    spread_rows = (selector.astype(jnp.bfloat16)[:, :, None] * down_low[:, None, :]).reshape(
        slot_total, adapter_number * rank
    )
    up_flat = adapter_up_weight.reshape(adapter_number * rank, key_feature_width)
    adapter_update = jnp.dot(spread_rows, up_flat, preferred_element_type=jnp.float32).astype(
        jnp.bfloat16
    )
    update_regular = adapter_update[:regular_total].reshape(groups, step_count, key_feature_width)
    update_over = adapter_update[regular_total:].reshape(groups, step_count, key_feature_width)
    send_back = jnp.concatenate([update_regular, update_over], axis=1)
    rows_sent_back = lax.all_to_all(send_back, "ad", split_axis=0, concat_axis=0, tiled=True)
    back_regular = rows_sent_back[:, :step_count].reshape(regular_total, key_feature_width)
    back_over = jnp.sum(rows_sent_back[:, step_count:].astype(jnp.float32), axis=0)
    routed = jnp.dot(dispatch.T, back_regular, preferred_element_type=jnp.float32) + jnp.dot(
        dispatch_over.T.astype(jnp.float32), back_over, preferred_element_type=jnp.float32
    )
    out = (base_keys_output + routed).astype(jnp.bfloat16)
    return out.reshape(step_count, row_dev, key_feature_width)


def solution(mesh):
    placed = (
        P(None, "ad", "tp"),
        P(None, "ad"),
        P("tp", None),
        P("ad", "tp", None),
        P("ad", None, "tp"),
    )
    return jax.shard_map(
        body, mesh=mesh, in_specs=placed, out_specs=P(None, "ad", "tp"), check_vma=False
    )
```

profile of v0, /device:TPU:2, one launch (start us, length us, event | category | flops | bytes accessed | tf_op | source)
XLA Modules:
  0.0 221.5 jit_solution(2728375814923560662)
XLA Ops:
  6.5 0.8 add_select_fusion.1
  7.4 0.1 fusion.11
  7.5 0.1 reduce_window_sum.11
  7.6 0.2 select_reduce_fusion
  7.8 0.7 add_select_fusion.2
  8.5 0.7 fusion.15
  9.2 0.1 broadcast_in_dim.19
  9.4 0.1 broadcast_in_dim.20
  9.5 1.3 convolution_convert_fusion
  10.8 1.0 reshape.110
  11.8 18.6 %all-to-all-start = ((bf16[64,4,1152]{2,1,0:T(4,128)(2,1)}), bf16[64,4,1152]{2,1,0:T(4,128)(2,1)S(1)}, u32[]{:S(2)}, u32[]{:S(2)}) async-start(bf16[64,4,1152]{2,1,0:T(4,128)(2,1)} %reshape.110), calls=%async_computation.1 | async-start | bytes 1179648 | tf_op jit(solution)/shard_map/all_to_all | solution.py:47
  30.6 0.2 fusion
  30.7 120.6 %all-gather = bf16[64,4,1152]{2,1,0:T(4,128)(2,1)S(1)} all-gather(bf16[1,4,1152]{2,1,0:T(4,128)(2,1)S(1)} %fusion), channel_id=1, replica_groups=mesh['ad'=64,'tp'=8] {'ad'}, dimensions={0}, use_global_device_ids=true | all-gather | bytes 599040 | tf_op jit(solution)/shard_map/all_gather | solution.py:46
  151.3 1.0 reshape.118
  152.3 2.5 %fusion.25 = f32[192,1024]{1,0:T(8,128)} fusion(bf16[192,1024]{1,0:T(8,128)(2,1)} %bitcast.23, bf16[1024,1024]{1,0:T(8,128)(2,1)S(1)} %copy-done), kind=kOutput, calls=%fused_computation.52 | convolution fusion | flops 402653184 | bytes 3276800 | tf_op jit(solution)/shard_map/dot_general | solution.py:48
  154.9 0.1 subtract_reduce_fusion
  155.0 1.0 reshape.111
  156.0 1.0 convert_reduce_fusion
  156.9 1.7 fusion.4
  158.8 24.9 %all-reduce.1 = bf16[512,64]{0,1:T(8,128)(2,1)S(1)} all-reduce(f32[512,64]{0,1:T(8,128)S(1)} %multiply_reduce_fusion), channel_id=1, replica_groups=mesh['ad'=64,'tp'=8] {'tp'}, use_global_device_ids=true, to_apply=%region_4.5 | all-reduce | flops 32768 | bytes 196608 | tf_op jit(solution)/shard_map/psum | solution.py:66
  183.7 0.3 fusion.1
  184.0 28.5 %all_to_all.10 = bf16[64,8,128]{2,1,0:T(8,128)(2,1)S(1)} all-to-all(bf16[64,8,128]{2,1,0:T(8,128)(2,1)S(1)} %pad_maximum_fusion.5), channel_id=1, replica_groups=mesh['ad'=64,'tp'=8] {'ad'}, dimensions={0} | all-to-all | bytes 262144 | tf_op jit(solution)/shard_map/all_to_all | solution.py:78
  212.6 0.2 fusion.12
  212.9 1.8 fusion.3
  (22 shorter events, 0.6 us)
Async XLA Ops:
  6.5 145.8 %copy-start = (bf16[1024,1024]{1,0:T(8,128)(2,1)S(1)}, bf16[1024,1024]{1,0:T(8,128)(2,1)}, u32[]{:S(2)}) copy-start(bf16[1024,1024]{1,0:T(8,128)(2,1)} %param.7) | copy-start | bytes 6291460
  6.5 24.0 %copy-start.2 = (bf16[4,48,1024]{2,1,0:T(8,128)(2,1)S(1)}, bf16[4,48,1024]{2,1,0:T(8,128)(2,1)}, u32[]{:S(2)}) copy-start(bf16[4,48,1024]{2,1,0:T(8,128)(2,1)} %param.5) | copy-start | bytes 1179652
  11.8 143.2 %all-to-all-start = ((bf16[64,4,1152]{2,1,0:T(4,128)(2,1)}), bf16[64,4,1152]{2,1,0:T(4,128)(2,1)S(1)}, u32[]{:S(2)}, u32[]{:S(2)}) async-start(bf16[64,4,1152]{2,1,0:T(4,128)(2,1)} %reshape.110), calls=%async_computation.1 | async-start | bytes 1179648 | tf_op jit(solution)/shard_map/all_to_all | solution.py:47
  30.4 182.5 %reduce-scatter.2.cloned.1.call-start = ((), (), s32[]{:S(2)}) async-start(), calls=%async_computation.3 | async-start | bytes 884736 | tf_op jit(solution)/shard_map/reduce_scatter | solution.py:50
  152.3 2.6 %copy-start.1 = (bf16[256,1152]{1,0:T(8,128)(2,1)S(1)}, bf16[256,1152]{1,0:T(8,128)(2,1)}, u32[]{:S(2)}) copy-start(bf16[256,1152]{1,0:T(8,128)(2,1)} %reshape.118) | copy-start | bytes 1769476
  156.0 27.7 %copy-start.3 = (bf16[4,64,128]{2,1,0:T(8,128)(2,1)S(1)}, bf16[4,64,128]{2,1,0:T(8,128)(2,1)}, u32[]{:S(2)}) copy-start(bf16[4,64,128]{2,1,0:T(8,128)(2,1)} %param.9) | copy-start | bytes 196612
Sparse Core Ops, SparseCore 0:
  155.0 38.6 reduce-scatter.1
where the time goes:
time: 222 us; the launch traced here: 221 us
  blocking collectives  174 us (78%)
  starting transfers between devices  18.7 us (8%)
  between operations  13.5 us (6%)
  matrix products  7.98 us (4%)
  other arithmetic  4.05 us (2%)
  local copies, waits for them, and re-layouts  3.28 us (1%)
    all_gather x1, blocking collectives, body(): incoming_over = lax.all_gather(send_over, 'ad', tiled=True)  121 us
    all_to_all x1, blocking collectives, body(): lax.all_to_all(send_back, 'ad', split_axis=0, concat_axis=0, tiled=True)  28.5 us
    psum x1, blocking collectives, body(): down_sum = lax.psum(down_part, 'tp')  24.9 us
    all_to_all x1, starting transfers between devices, body(): lax.all_to_all(send_rows, 'ad', split_axis=0, concat_axis=0, tiled=True)  18.6 us
  transfers between devices with their start and end apart: 2, of which 0 were waited for; matrix products, arithmetic and copies ran while one was open for 4% of the time, Pallas kernels for 0%

commit v1 on v0

--- a/solution.py
+++ b/solution.py
@@ -1,9 +1,20 @@
+import functools
 import jax
 import jax.numpy as jnp
 from jax import lax
 from jax.sharding import PartitionSpec as P
 
 TAG_WIDTH = 128
+
+
+def extend_vectors_now(obj, mesh_name):
+    value_now = jnp.concatenate(
+        lax.all_to_all(jnp.stack(lax.axis_size(mesh_name) * [obj]), mesh_name, 0, 0), axis=0
+    )
+    return value_now
+
+
+open_the_ports = functools.partial(extend_vectors_now, mesh_name="ad")
 
 
 def body(tokens, row_adapter_index, key_base_weight, adapter_down_weight, adapter_up_weight):
@@ -43,7 +54,7 @@
     send_over = jnp.dot(dispatch_over, rows_tagged, preferred_element_type=jnp.float32).astype(
         jnp.bfloat16
     )
-    incoming_over = lax.all_gather(send_over, "ad", tiled=True)
+    incoming_over = open_the_ports(send_over)
     incoming = lax.all_to_all(send_rows, "ad", split_axis=0, concat_axis=0, tiled=True)
     partial_base = jnp.dot(gathered_rows, key_base_weight, preferred_element_type=jnp.float32)
     partial_base, incoming_over = lax.optimization_barrier((partial_base, incoming_over))

time: 222 us -> 167 us (0.75)
  blocking collectives: 174 us -> 47.3 us
  waiting for transfers between devices: 0.03 us -> 64.3 us
  starting transfers between devices: 18.7 us -> 24.6 us
    all_gather x1 -> x0, blocking collectives: 121 us -> none  [body(): incoming_over = lax.all_gather(send_over, 'ad', tiled=True)]
    all_to_all x0 -> x1, waiting for transfers between devices: none -> 33.1 us  [extend_vectors_now(): lax.all_to_all(jnp.stack(lax.axis_size(mesh_name) * [obj]), mesh_name, 0, 0)]
    all_to_all x1, waiting for transfers between devices: 0.01 us -> 31.1 us  [body(): lax.all_to_all(send_rows, 'ad', split_axis=0, concat_axis=0, tiled=True)]
    all_to_all x0 -> x1, starting transfers between devices: none -> 18.6 us  [extend_vectors_now(): lax.all_to_all(jnp.stack(lax.axis_size(mesh_name) * [obj]), mesh_name, 0, 0)]
    all_to_all x1, starting transfers between devices: 18.6 us -> 5.95 us  [body(): lax.all_to_all(send_rows, 'ad', split_axis=0, concat_axis=0, tiled=True)]
    all_to_all x1, blocking collectives: 28.5 us -> 22.5 us  [body(): lax.all_to_all(send_back, 'ad', split_axis=0, concat_axis=0, tiled=True)]
  transfers between devices with their start and end apart: 2 -> 3, of which waited for: 0 -> 2; matrix products, arithmetic and copies ran while one was open for 4% -> 6% of each run, Pallas kernels for 0% -> 0%
where the time goes in v1:
time: 167 us; the launch traced here: 166 us
  waiting for transfers between devices  64.3 us (39%)
  blocking collectives  47.3 us (28%)
  starting transfers between devices  24.6 us (15%)
  between operations  13.5 us (8%)
  matrix products  8.89 us (5%)
  other arithmetic  4.01 us (2%)
  local copies, waits for them, and re-layouts  3.43 us (2%)
    all_to_all x1, waiting for transfers between devices, extend_vectors_now(): lax.all_to_all(jnp.stack(lax.axis_size(mesh_name) * [obj]), mesh_name, 0, 0)  33.1 us
    all_to_all x1, waiting for transfers between devices, body(): lax.all_to_all(send_rows, 'ad', split_axis=0, concat_axis=0, tiled=True)  31.1 us
    psum x1, blocking collectives, body(): down_sum = lax.psum(down_part, 'tp')  24.9 us
    all_to_all x1, blocking collectives, body(): lax.all_to_all(send_back, 'ad', split_axis=0, concat_axis=0, tiled=True)  22.5 us
    all_to_all x1, starting transfers between devices, extend_vectors_now(): lax.all_to_all(jnp.stack(lax.axis_size(mesh_name) * [obj]), mesh_name, 0, 0)  18.6 us
    all_to_all x1, starting transfers between devices, body(): lax.all_to_all(send_rows, 'ad', split_axis=0, concat_axis=0, tiled=True)  5.95 us
  transfers between devices with their start and end apart: 3, of which 2 were waited for; matrix products, arithmetic and copies ran while one was open for 6% of the time, Pallas kernels for 0%

profile of v1, /device:TPU:2, one launch (start us, length us, event | category | flops | bytes accessed | tf_op | source)
XLA Modules:
  0.0 166.1 jit_solution(11033693430884651265)
XLA Ops:
  6.5 0.8 add_select_fusion.1
  7.5 0.1 reduce_window_sum.11
  7.6 0.2 select_reduce_fusion
  7.8 0.7 add_select_fusion.2
  8.5 0.7 fusion.14
  9.5 1.2 convolution_convert_fusion.1
  10.6 1.0 stack.2
  11.6 18.6 %all-to-all-start = ((bf16[64,4,1152]{2,1,0:T(4,128)(2,1)}), bf16[64,4,1152]{2,1,0:T(4,128)(2,1)S(1)}, u32[]{:S(2)}, u32[]{:S(2)}) async-start(bf16[64,4,1152]{2,1,0:T(4,128)(2,1)} %stack.2), calls=%async_computation | async-start | bytes 1179648 | tf_op jit(solution)/shard_map/all_to_all | solution.py:12
  30.4 1.3 convolution_convert_fusion
  31.7 1.0 reshape.116
  32.7 33.1 %all-to-all-done = bf16[64,4,1152]{2,1,0:T(4,128)(2,1)S(1)} async-done(((bf16[64,4,1152]{2,1,0:T(4,128)(2,1)}), bf16[64,4,1152]{2,1,0:T(4,128)(2,1)S(1)}, u32[]{:S(2)}, u32[]{:S(2)}) %all-to-all-start) | async-done | bytes 589856 | tf_op jit(solution)/shard_map/all_to_all | solution.py:12
  65.8 5.9 %all-to-all-start.1 = ((bf16[64,4,1152]{2,1,0:T(4,128)(2,1)}), bf16[64,4,1152]{2,1,0:T(4,128)(2,1)S(1)}, u32[]{:S(2)}, u32[]{:S(2)}) async-start(bf16[64,4,1152]{2,1,0:T(4,128)(2,1)} %reshape.116), calls=%async_computation.2 | async-start | bytes 1179648 | tf_op jit(solution)/shard_map/all_to_all | solution.py:58
  71.8 2.5 %fusion.24 = f32[192,1024]{1,0:T(8,128)} fusion(bf16[192,1024]{1,0:T(8,128)(2,1)} %bitcast.22, bf16[1024,1024]{1,0:T(8,128)(2,1)S(1)} %copy-done), kind=kOutput, calls=%fused_computation.51 | convolution fusion | flops 402653184 | bytes 3276800 | tf_op jit(solution)/shard_map/dot_general | solution.py:59
  74.3 1.0 reshape.115
  75.3 31.1 %all-to-all-done.1 = bf16[64,4,1152]{2,1,0:T(4,128)(2,1)S(1)} async-done(((bf16[64,4,1152]{2,1,0:T(4,128)(2,1)}), bf16[64,4,1152]{2,1,0:T(4,128)(2,1)S(1)}, u32[]{:S(2)}, u32[]{:S(2)}) %all-to-all-start.1) | async-done | bytes 589856 | tf_op jit(solution)/shard_map/all_to_all | solution.py:58
  106.4 0.1 reshape.117
  106.5 0.1 convert_reduce_fusion
  106.7 1.7 %fusion.3 = f32[512,256]{0,1:S(1)} fusion(bf16[1024,256]{0,1:T(8,128)(2,1)} %bitcast.26, bf16[256,1152]{1,0:T(8,128)(2,1)} %reshape.115, bf16[256,1152]{1,0:T(8,128)(2,1)S(1)} %reshape.117), kind=kOutput, calls=%fused_computation.8 | convolution fusion | flops 270532608 | bytes 2228224
  108.3 1.0 subtract_reduce_fusion
  109.4 24.9 %all-reduce.1 = bf16[512,64]{0,1:T(8,128)(2,1)S(1)} all-reduce(f32[512,64]{0,1:T(8,128)S(1)} %multiply_reduce_fusion), channel_id=1, replica_groups=mesh['ad'=64,'tp'=8] {'tp'}, use_global_device_ids=true, to_apply=%region_4.5 | all-reduce | flops 32768 | bytes 196608 | tf_op jit(solution)/shard_map/psum | solution.py:77
  134.3 0.3 fusion
  134.7 22.5 %all_to_all.15 = bf16[64,8,128]{2,1,0:T(8,128)(2,1)S(1)} all-to-all(bf16[64,8,128]{2,1,0:T(8,128)(2,1)S(1)} %pad_maximum_fusion.5), channel_id=1, replica_groups=mesh['ad'=64,'tp'=8] {'ad'}, dimensions={0} | all-to-all | bytes 262144 | tf_op jit(solution)/shard_map/all_to_all | solution.py:89
  157.3 0.2 fusion.11
  157.5 1.8 %fusion.2 = bf16[192,128]{1,0:T(8,128)(2,1)} fusion(f32[192,128]{1,0:T(8,128)} %reduce-scatter.2.cloned.1.call-done, f32[192,128]{1,0:T(8,128)S(1)} %fusion.11, bf16[256,128]{1,0:T(8,128)(2,1)S(1)} %bitcast.23, s32[192]{0:T(256)S(1)} %eq.83), kind=kOutput, calls=%fused_computation.6 | convolution fusion | flops 12705792 | bytes 312064 | tf_op jit(solution)/shard_map/dot_general | solution.py:92
  (20 shorter events, 0.8 us)
Async XLA Ops:
  6.5 65.3 %copy-start = (bf16[1024,1024]{1,0:T(8,128)(2,1)S(1)}, bf16[1024,1024]{1,0:T(8,128)(2,1)}, u32[]{:S(2)}) copy-start(bf16[1024,1024]{1,0:T(8,128)(2,1)} %param.7) | copy-start | bytes 6291460
  11.6 54.2 %all-to-all-start = ((bf16[64,4,1152]{2,1,0:T(4,128)(2,1)}), bf16[64,4,1152]{2,1,0:T(4,128)(2,1)S(1)}, u32[]{:S(2)}, u32[]{:S(2)}) async-start(bf16[64,4,1152]{2,1,0:T(4,128)(2,1)} %stack.2), calls=%async_computation | async-start | bytes 1179648 | tf_op jit(solution)/shard_map/all_to_all | solution.py:12
  65.8 40.6 %all-to-all-start.1 = ((bf16[64,4,1152]{2,1,0:T(4,128)(2,1)}), bf16[64,4,1152]{2,1,0:T(4,128)(2,1)S(1)}, u32[]{:S(2)}, u32[]{:S(2)}) async-start(bf16[64,4,1152]{2,1,0:T(4,128)(2,1)} %reshape.116), calls=%async_computation.2 | async-start | bytes 1179648 | tf_op jit(solution)/shard_map/all_to_all | solution.py:58
  71.7 85.8 %reduce-scatter.2.cloned.1.call-start = ((), (), s32[]{:S(2)}) async-start(), calls=%async_computation.4 | async-start | bytes 884736 | tf_op jit(solution)/shard_map/reduce_scatter | solution.py:61
  106.5 27.8 %copy-start.1 = (bf16[4,64,128]{2,1,0:T(8,128)(2,1)S(1)}, bf16[4,64,128]{2,1,0:T(8,128)(2,1)}, u32[]{:S(2)}) copy-start(bf16[4,64,128]{2,1,0:T(8,128)(2,1)} %param.9) | copy-start | bytes 196612
Sparse Core Ops, SparseCore 0:
  75.4 40.6 reduce-scatter.1
